TPU v7x, 32 devices: a whole 2x2x4 slice. The times are simulated.
32 devices in a mesh: date: 2 (over x), blk: 8 (over z, y), sect: 2 (over core).
Axes of the slice: x: 2, y: 2, z: 4, core: 2. Of those that a mesh axis runs over, the one named last changes fastest.
Arguments:
- obs_weight: bfloat16 [16, 2, 512, 128], P(('date', 'blk'), 'sect'), parts along dimension 0, may hold values from -4 to 4
- obs_frac: bfloat16 [16, 2, 2, 512], P(('date', 'blk'), 'sect'), parts along dimension 0, may hold values from 0 to 1
- obs_cell: int32 [16, 2, 512], P(('date', 'blk'), 'sect'), parts along dimension 0, may hold values from 0 to 127
- obs_level: int32 [16, 2, 512], P(('date', 'blk'), 'sect'), parts along dimension 0, may hold values from 0 to 63
- obs_count: int32 [16, 2], P(('date', 'blk'), 'sect'), parts along dimension 0, may hold values from 1 to 512, as said below
- reach: int32 [16, 2], P(('date', 'blk')), parts along dimension 0, may hold values from 0 to 3, as said below
- length_x: float32 [64], replicated, may hold values from 0.5 to 2
- length_y: float32 [64], replicated, may hold values from 0.1 to 0.5
- tilt: float32 [64], replicated, may hold values from -0.7 to 0.7
- vert_len: float32 [64], replicated, may hold values from 1.5 to 12
- balance: float32 [64, 64], replicated, may hold values from -0.75 to 0.75
Outputs:
- increment: float32 [64, 2048, 128], P('sect', ('date', 'blk')), parts along dimension 1
There are 2 independent parts, one for each index of `date`. A program takes and returns all parts, laid end to end along the dimension named above; an argument that names none is the same for every part. Nothing has to cross between parts.
Inputs may be any that keep to these rules, and one draw needn't show every extreme that they name: `obs_count`: 512 is reached in every draw. `reach`: 0 and 3 both occur in every draw.
All inputs are finite; a program needn't handle non-finite values.
Results may differ from a plain program's by a relative error of at most 0.0029.
Values may be sent and summed in bfloat16 or wider, within the bound.
No kernel may reach another device: no remote copies, remote signals or barrier semaphores. Data moves between devices by JAX's collectives and lax.ppermute only.
A program may use at most 64 MiB of HBM per device.

v0:
```python
import functools
import jax
import jax.numpy as jnp
from jax import lax
from jax.experimental import pallas as pl
from jax.experimental.pallas import tpu as pltpu
from jax.sharding import PartitionSpec as P

GX = 8
GY = 16
G_DEV = GX * GY
TILE = 128
JOIN = 2
GROUP = 16
F32 = jnp.float32
BF16 = jnp.bfloat16
VMEM = pl.BlockSpec(memory_space=pltpu.VMEM)
SMEM = pl.BlockSpec(memory_space=pltpu.SMEM)
PARAMS = pltpu.CompilerParams(vmem_limit_bytes=20 << 20)


def pack_kernel(
    count_ref,
    reach_hbm,
    weight_hbm,
    frac_hbm,
    cell_hbm,
    level_hbm,
    lx_hbm,
    ly_hbm,
    tl_hbm,
    vl_hbm,
    balance_hbm,
    out_ref,
    scale_ref,
    left_ref,
    reach_ref,
    weight_ref,
    frac_ref,
    cell_ref,
    level_ref,
    lx_ref,
    ly_ref,
    tl_ref,
    vl_ref,
    balance_ref,
    sems,
):
    pairs = (
        (weight_hbm, weight_ref),
        (frac_hbm, frac_ref),
        (cell_hbm, cell_ref),
        (level_hbm, level_ref),
        (reach_hbm, reach_ref),
        (lx_hbm, lx_ref),
        (ly_hbm, ly_ref),
        (tl_hbm, tl_ref),
        (vl_hbm, vl_ref),
        (balance_hbm, balance_ref),
    )
    copies = [pltpu.make_async_copy(src, dst, sems.at[i]) for i, (src, dst) in enumerate(pairs)]
    for copy in copies:
        copy.start()
    for copy in copies:
        copy.wait()
    capacity = weight_ref.shape[2]
    chunks = capacity // TILE
    levels = lx_ref.shape[1]
    half = levels // 2
    count = count_ref[0, 0]
    row = lax.broadcasted_iota(jnp.int32, (capacity, TILE), 0)
    weight = weight_ref[0, 0].astype(F32)
    out_ref[0:capacity, :] = jnp.where(row < count, weight, 0.0).astype(BF16)
    fraction = frac_ref[0, 0].astype(F32)
    cell = cell_ref[0].astype(F32)
    level = level_ref[0].astype(F32)
    rows = []
    for table in (fraction[0:1], fraction[1:2], cell, level):
        for i in range(chunks):
            rows.append(table[:, i * TILE : (i + 1) * TILE])
    out_ref[capacity : capacity + 4 * chunks, :] = jnp.concatenate(rows, 0).astype(BF16)
    live = (count + TILE - 1) // TILE
    code = live + 8 * (reach_ref[0, 0] + 4 * reach_ref[0, 1])
    tail = out_ref.shape[0] - capacity - 4 * chunks
    out_ref[capacity + 4 * chunks :, :] = jnp.full((tail, TILE), code, jnp.int32).astype(F32).astype(BF16)
    inv_x = 1.0 / lx_ref[...]
    inv_y = 1.0 / ly_ref[...]
    tilt = tl_ref[...]
    lines = [inv_x, tilt * inv_y, (1.0 - tilt * tilt) * inv_y * inv_y, 1.0 / vl_ref[...]]
    scale_ref[...] = jnp.transpose(jnp.concatenate(lines + lines, 0))
    mine = lax.axis_index("sect")
    matrix = jnp.concatenate(
        [
            balance_ref[pl.ds(pl.multiple_of(mine * half, half), half), :],
            balance_ref[pl.ds(pl.multiple_of((1 - mine) * half, half), half), :],
        ],
        0,
    )
    high = matrix.astype(BF16)
    low = (matrix - high.astype(F32)).astype(BF16)
    left_ref[...] = jnp.concatenate([high, low, high], 1)


def pack(obs_count, reach, obs_weight, obs_frac, obs_cell, obs_level, scales, balance):
    capacity = obs_weight.shape[2]
    levels = balance.shape[0]
    rows = capacity + 4 * (capacity // TILE) + 16
    operands = [obs_count, reach, obs_weight, obs_frac, obs_cell, obs_level, *scales, balance]
    operands[1:] = [pltpu.with_memory_space_constraint(v, pltpu.HBM) for v in operands[1:]]
    spaces = [pltpu.SMEM] + [pltpu.VMEM] * 9
    return pl.pallas_call(
        pack_kernel,
        out_shape=(
            jax.ShapeDtypeStruct((rows, TILE), BF16),
            jax.ShapeDtypeStruct((levels, 8), F32),
            jax.ShapeDtypeStruct((levels, 3 * levels), BF16),
        ),
        in_specs=[SMEM] + [pl.BlockSpec(memory_space=pltpu.HBM)] * (len(operands) - 1),
        out_specs=(VMEM, VMEM, VMEM),
        scratch_shapes=[space(v.shape, v.dtype) for space, v in zip(spaces, operands[1:])]
        + [pltpu.SemaphoreType.DMA((len(operands) - 1,))],
        compiler_params=PARAMS,
    )(*operands)


def gather_chunks(packets, offsets, capacity, w_all, ox_all, oy_all, le_all, order):
    chunks = capacity // TILE
    filled = jnp.int32(0)
    for i, (packet, offset) in enumerate(zip(packets, offsets)):
        w_all[i * capacity : (i + 1) * capacity, :] = packet[0:capacity, :]
        place = packet[capacity : capacity + 4 * chunks, :].astype(F32)
        fx, fy, cell, level = (place[t * chunks : (t + 1) * chunks] for t in range(4))
        cx = jnp.floor(cell * (1.0 / GY))
        cy = cell - cx * GY
        shift = jnp.full((1, TILE), offset, jnp.int32).astype(F32)
        ox_all[i * chunks : (i + 1) * chunks, :] = (cx + fx) * (1.0 / GX) - shift
        oy_all[i * chunks : (i + 1) * chunks, :] = (cy + fy) * (1.0 / GY)
        le_all[i * chunks : (i + 1) * chunks, :] = level
        tail = packet[capacity + 4 * chunks :, :].astype(F32)
        code = jnp.max(tail).astype(jnp.int32)
        live = code & 7
        below = (code >> 3) & 3
        above = (code >> 5) & 3
        used = jnp.where((offset <= above) & (-offset <= below), live, 0)
        for c in range(chunks):
            order[filled + c] = i * chunks + c
        filled = filled + used
    blank = len(packets) * chunks
    w_all[blank * TILE : (blank + 1) * TILE, :] = jnp.zeros((TILE, TILE), BF16)
    for ref in (ox_all, oy_all, le_all):
        ref[blank : blank + 8, :] = jnp.zeros((8, TILE), F32)
    for c in range(JOIN - 1):
        order[filled + c] = blank
    return filled


def spread(filled, scale, acc, w_all, ox_all, oy_all, le_all, order, wq, dxs, dys, dzs, sx, ys, zs):
    levels = scale.shape[0]
    inv_x = scale[:, 0:1]
    tilt_y = scale[:, 1:2]
    rest_y = scale[:, 2:3]
    inv_v = scale[:, 3:4]
    height = lax.broadcasted_iota(jnp.int32, (levels, 1), 0).astype(F32)
    grid_x = (lax.broadcasted_iota(jnp.int32, (GX, 1), 0).astype(F32) + 0.5) / GX
    grid_y = (lax.broadcasted_iota(jnp.int32, (GY, 1), 0).astype(F32) + 0.5) / GY

    def join(q, _):
        picks = [order[q * JOIN + i] for i in range(JOIN)]
        for i, r in enumerate(picks):
            wq[i * TILE : (i + 1) * TILE, :] = w_all[pl.ds(pl.multiple_of(r * TILE, TILE), TILE), :]

        def lanes(ref):
            return jnp.concatenate([ref[pl.ds(r, 1), :] for r in picks], 1)

        dxs[...] = grid_x - lanes(ox_all)
        dy = grid_y - lanes(oy_all)
        dys[...] = dy
        dzs[...] = dy * dy
        sep = (height - lanes(le_all)) * inv_v
        root = lax.rsqrt(lax.rsqrt(1.0 + sep * sep))
        full = root * root
        sx[...] = root * inv_x
        sy_all = root * tilt_y
        sz_all = full * rest_y
        right = wq[...]
        for first in range(0, levels, GROUP):
            span = slice(first, first + GROUP)
            for i in range(GY):
                ys[i, span, :] = sy_all[span] * dys[i : i + 1, :]
                zs[i, span, :] = sz_all[span] * dzs[i : i + 1, :] + full[span]
            rows = []
            for i in range(GX):
                xv = sx[span, :] * dxs[i : i + 1, :]
                for j in range(GY):
                    a = xv + ys[j, span, :]
                    y = a * a + zs[j, span, :]
                    rows.append((1.0 / (y * y)).astype(BF16))
            term = jnp.dot(jnp.concatenate(rows, 0), right, preferred_element_type=F32)
            for j in range(G_DEV):
                at = slice(j * levels + first, j * levels + first + GROUP)
                acc[at, :] += term[j * GROUP : (j + 1) * GROUP]
        return 0

    lax.fori_loop(0, (filled + JOIN - 1) // JOIN, join, 0)


def balance_step(left_ref, acc, own, other, base):
    levels = left_ref.shape[0]
    half = levels // 2
    left = left_ref[...]
    for j in range(0, own.shape[0], 2):
        value = jnp.concatenate(
            [acc[(base + j + n) * levels : (base + j + n + 1) * levels, :] for n in range(2)], 1
        )
        big = value.astype(BF16)
        small = (value - big.astype(F32)).astype(BF16)
        right = jnp.concatenate([big, big, small], 0)
        result = jnp.dot(left, right, preferred_element_type=F32)
        for n in range(2):
            own[j + n] = result[0:half, n * TILE : (n + 1) * TILE]
            other[j + n] = result[half:, n * TILE : (n + 1) * TILE].astype(BF16)


def rest_kernel(left, acc, own, other):
    balance_step(left, acc, own, other, G_DEV // 2)


def main_kernel(*refs, hops, capacity, first, last):
    refs = list(refs)
    scale = refs.pop(0)
    if not first:
        refs.pop(0)
    rows = capacity + 4 * (capacity // TILE) + 16
    packets = []
    while len(packets) < len(hops):
        group = refs.pop(0)
        for i in range(group.shape[0] // rows):
            packets.append(group.at[i * rows : (i + 1) * rows, :])
    left = refs.pop(0) if last else None
    acc = refs.pop(0)
    if last:
        own, other = refs[:2]
        refs = refs[2:]
    if first:
        acc[...] = jnp.zeros(acc.shape, F32)
    parity = lax.rem(lax.axis_index("blk"), 2)
    offsets = [even if even == odd else jnp.where(parity == 0, even, odd) for even, odd in hops]
    filled = gather_chunks(packets, offsets, capacity, *refs[:5])
    spread(filled, scale, acc, *refs)
    if last:
        balance_step(left, acc, own, other, 0)


def main_call(scale, acc, packets, hops, capacity, left=None):
    first = acc is None
    last = left is not None
    levels = scale.shape[0]
    chunks = capacity // TILE
    slots = len(hops) * chunks + 8
    operands = [scale]
    aliases = {}
    if not first:
        aliases = {1: 0}
        operands.append(acc)
    operands += list(packets)
    out_shape = [jax.ShapeDtypeStruct((levels * G_DEV, TILE), F32)]
    if last:
        operands.append(left)
        half = levels // 2
        out_shape.append(jax.ShapeDtypeStruct((G_DEV // 2, half, TILE), F32))
        out_shape.append(jax.ShapeDtypeStruct((G_DEV // 2, half, TILE), BF16))
    width = JOIN * TILE
    scratch = [pltpu.VMEM(((len(hops) * chunks + 1) * TILE, TILE), BF16)]
    scratch += [pltpu.VMEM((slots, TILE), F32)] * 3
    scratch += [pltpu.SMEM((slots + JOIN,), jnp.int32), pltpu.VMEM((width, TILE), BF16)]
    scratch += [pltpu.VMEM((n, width), F32) for n in (GX, GY, GY, levels)]
    scratch += [pltpu.VMEM((GY, levels, width), F32)] * 2
    return pl.pallas_call(
        functools.partial(main_kernel, hops=hops, capacity=capacity, first=first, last=last),
        out_shape=out_shape,
        in_specs=[VMEM] * len(operands),
        out_specs=[VMEM] * len(out_shape),
        scratch_shapes=scratch,
        input_output_aliases=aliases,
        compiler_params=PARAMS,
    )(*operands)


def finish_kernel(*refs, base):
    own, other = refs[:2]
    out, total, sems = refs[-3:]
    parts = sems.shape[0]
    count = own.shape[0]
    width = count // parts
    copies = []
    for p in range(parts):
        for j in range(p * width, (p + 1) * width):
            total[j] = own[j] + other[j].astype(F32)
        for j in range(p * width, (p + 1) * width):
            copies.append(pltpu.make_async_copy(total.at[j], out.at[:, base + j, :], sems.at[p]))
            copies[-1].start()
    for copy in copies:
        copy.wait()


def finish(own, other, out, base):
    count, half, width = own.shape
    operands = [own, other]
    specs = [VMEM, VMEM]
    aliases = {}
    if out is not None:
        operands.append(out)
        specs.append(pl.BlockSpec(memory_space=pltpu.HBM))
        aliases = {2: 0}
    return pl.pallas_call(
        functools.partial(finish_kernel, base=base),
        out_shape=jax.ShapeDtypeStruct((half, G_DEV, width), F32),
        in_specs=specs,
        out_specs=pl.BlockSpec(memory_space=pltpu.HBM),
        scratch_shapes=[pltpu.VMEM((count, half, width), F32), pltpu.SemaphoreType.DMA((4,))],
        input_output_aliases=aliases,
        compiler_params=PARAMS,
    )(*operands)


def shards(
    obs_weight,
    obs_frac,
    obs_cell,
    obs_level,
    obs_count,
    reach,
    length_x,
    length_y,
    tilt,
    vert_len,
    balance,
):
    levels = balance.shape[0]
    capacity = obs_weight.shape[2]
    blocks = lax.axis_size("blk")
    scales = [v.reshape(1, levels) for v in (length_x, length_y, tilt, vert_len)]
    packet, scale, left = pack(
        obs_count, reach, obs_weight, obs_frac, obs_cell, obs_level, scales, balance
    )

    def move(value, where):
        return lax.ppermute(value, "blk", [(i, where(i) % blocks) for i in range(blocks)])

    def swap(i):
        return i + 1 if i % 2 == 0 else i - 1

    up = move(packet, lambda i: i + 2)
    down = move(packet, lambda i: i - 2)
    near = move(packet, swap)
    cross = move(packet, lambda i: i - 3 if i % 2 == 0 else i + 3)
    (acc,) = main_call(scale, None, (packet,), ((0, 0),), capacity)
    up, down, acc = lax.optimization_barrier((up, down, acc))
    sides = jnp.concatenate([up, down], 0)
    near_sides = move(sides, swap)
    (acc,) = main_call(scale, acc, (sides, near), ((2, 2), (-2, -2), (-1, 1)), capacity)
    cross, acc = lax.optimization_barrier((cross, acc))
    (acc,) = main_call(scale, acc, (cross,), ((3, -3),), capacity)
    near_sides, acc = lax.optimization_barrier((near_sides, acc))
    acc, own, other = main_call(scale, acc, (near_sides,), ((1, 3), (-3, -1)), capacity, left)
    half = levels // 2
    first_other = lax.ppermute(other, "sect", [(0, 1), (1, 0)])
    rest_own, rest_other = pl.pallas_call(
        rest_kernel,
        out_shape=(
            jax.ShapeDtypeStruct((G_DEV // 2, half, TILE), F32),
            jax.ShapeDtypeStruct((G_DEV // 2, half, TILE), BF16),
        ),
        in_specs=[VMEM, VMEM],
        out_specs=(VMEM, VMEM),
        compiler_params=PARAMS,
    )(left, acc)
    second_other = lax.ppermute(rest_other, "sect", [(0, 1), (1, 0)])
    out = finish(own, first_other, None, 0)
    out = finish(rest_own, second_other, out, G_DEV // 2)
    return out


def solution(mesh):
    placed = (
        P(("date", "blk"), "sect", None, None),
        P(("date", "blk"), "sect", None, None),
        P(("date", "blk"), "sect", None),
        P(("date", "blk"), "sect", None),
        P(("date", "blk"), "sect"),
        P(("date", "blk"), None),
        P(),
        P(),
        P(),
        P(),
        P(),
    )
    return jax.shard_map(
        shards,
        mesh=mesh,
        in_specs=placed,
        out_specs=P("sect", ("date", "blk"), None),
        check_vma=False,
    )
```

profile of v0, /device:TPU:27, one launch (start us, length us, event | category | flops | bytes accessed | tf_op | source)
XLA Modules:
  0.0 42.5 jit_solution(115058102367408816)
XLA Ops:
  0.7 1.2 %shard_map.109 = (bf16[544,128]{1,0:T(8,128)(2,1)S(1)}, f32[64,8]{1,0:T(8,128)S(1)}, bf16[64,192]{1,0:T(8,128)(2,1)S(1)}) custom-call(s32[1,1]{1,0:T(1,128)S(6)} %copy.21.count_ref, s32[1,2]{1,0:T(1,128)} %reach_hbm.1, bf16[1,1,512,128]{3,2,1,0:T(8,128)(2,1)} %weight_hbm.1, bf16[1,1,2,512]{3,2,1,0:T(2,128)(2,1)} %frac_hbm.1, s32[1,1,512]{2,1,0:T(1,128)} %cell_hbm.1, ...), custom_call_target="tpu_custom_call" | custom-call | tf_op jit(solution)/shard_map/pallas_call | solution.py:111
  1.9 0.2 collective-permute-start.1
  2.1 3.1 %collective-permute-start = (bf16[544,128]{1,0:T(8,128)(2,1)S(1)}, bf16[544,128]{1,0:T(8,128)(2,1)S(1)}, u32[]{:S(2)}, u32[]{:S(2)}) collective-permute-start(bf16[544,128]{1,0:T(8,128)(2,1)S(1)} %get-tuple-element.22.refs_1_), channel_id=1, source_target_pairs={{0,4},{2,6},{4,8},{6,10},{8,12},{10,14},{12,0},{14,2},{1,5},{3,7},... | collective-permute-start | bytes 417800 | tf_op jit(solution)/shard_map/ppermute | solution.py:348
  5.2 2.3 %shard_map.110.refs_1_ = f32[8192,128]{1,0:T(8,128)S(1)} custom-call(f32[64,8]{1,0:T(8,128)S(1)} %get-tuple-element.21.refs_0_, bf16[544,128]{1,0:T(8,128)(2,1)S(1)} %get-tuple-element.22.refs_1_), custom_call_target="tpu_custom_call" | custom-call | tf_op jit(solution)/shard_map/pallas_call | solution.py:278
  7.5 0.8 %collective-permute-done.1 = bf16[544,128]{1,0:T(8,128)(2,1)S(1)} collective-permute-done((bf16[544,128]{1,0:T(8,128)(2,1)S(1)}, bf16[544,128]{1,0:T(8,128)(2,1)S(1)}, u32[]{:S(2)}, u32[]{:S(2)}) %collective-permute-start.1) | collective-permute-done | bytes 139296 | tf_op jit(solution)/shard_map/ppermute | solution.py:348
  8.4 0.0 collective-permute-done
  8.4 1.3 %collective-permute-start.2 = (bf16[1088,128]{1,0:T(8,128)(2,1)S(1)}, bf16[1088,128]{1,0:T(8,128)(2,1)S(1)}, u32[]{:S(2)}, u32[]{:S(2)}) collective-permute-start(bf16[1088,128]{1,0:T(8,128)(2,1)S(1)} %constant_dynamic-update-slice_fusion.refs_2_), channel_id=1, source_target_pairs={{0,2},{2,0},{4,6},{6,4},{8,10},{10,8},{12,14},{14,12},{1,3},{3,1},... | collective-permute-start | bytes 835592 | tf_op jit(solution)/shard_map/ppermute | solution.py:348
  9.7 0.2 collective-permute-start.4
  9.9 4.2 %collective-permute-start.3 = (bf16[544,128]{1,0:T(8,128)(2,1)S(1)}, bf16[544,128]{1,0:T(8,128)(2,1)S(1)}, u32[]{:S(2)}, u32[]{:S(2)}) collective-permute-start(bf16[544,128]{1,0:T(8,128)(2,1)S(1)} %get-tuple-element.22.refs_1_), channel_id=1, source_target_pairs={{0,10},{2,8},{4,14},{6,12},{8,2},{10,0},{12,6},{14,4},{1,11},{3,9}... | collective-permute-start | bytes 417800 | tf_op jit(solution)/shard_map/ppermute | solution.py:348
  14.2 4.2 %collective-permute-done.4.refs_3_ = bf16[544,128]{1,0:T(8,128)(2,1)S(1)} collective-permute-done((bf16[544,128]{1,0:T(8,128)(2,1)S(1)}, bf16[544,128]{1,0:T(8,128)(2,1)S(1)}, u32[]{:S(2)}, u32[]{:S(2)}) %collective-permute-start.4) | collective-permute-done | bytes 139296 | tf_op jit(solution)/shard_map/ppermute | solution.py:348
  18.4 6.2 %shard_map.111.refs_1_ = f32[8192,128]{1,0:T(8,128)S(1)} custom-call(f32[64,8]{1,0:T(8,128)S(1)} %get-tuple-element.21.refs_0_, f32[8192,128]{1,0:T(8,128)S(1)} %shard_map.110.refs_1_, bf16[1088,128]{1,0:T(8,128)(2,1)S(1)} %constant_dynamic-update-slice_fusion.refs_2_, ...), custom_call_target="tpu_custom_call", output_to_operand_aliasing={{}: (1, {})} | custom-call | tf_op jit(solution)/shard_map/pallas_call | solution.py:278
  24.6 0.0 collective-permute-done.3.refs_2_
  24.6 0.1 shard_map.112.refs_1_
  24.7 0.0 collective-permute-done.2.refs_2_
  24.7 2.9 %shard_map.113 = (f32[8192,128]{1,0:T(8,128)S(1)}, f32[64,32,128]{2,1,0:T(8,128)S(1)}, bf16[64,32,128]{2,1,0:T(8,128)(2,1)S(1)}) custom-call(f32[64,8]{1,0:T(8,128)S(1)} %get-tuple-element.21.refs_0_, f32[8192,128]{1,0:T(8,128)S(1)} %shard_map.112.refs_1_, bf16[1088,128]{1,0:T(8,128)(2,1)S(1)} %collective-permute-done.2.refs_2_, ...), custom_call_target="tpu_custom_call", output_to_operand_aliasing={{0}: (1, {})} | custom-call | tf_op jit(solution)/shard_map/pallas_call | solution.py:278
  27.6 11.2 %collective-permute-start.6 = (bf16[64,32,128]{2,1,0:T(8,128)(2,1)S(1)}, bf16[64,32,128]{2,1,0:T(8,128)(2,1)S(1)}, u32[]{:S(2)}, u32[]{:S(2)}) collective-permute-start(bf16[64,32,128]{2,1,0:T(8,128)(2,1)S(1)} %get-tuple-element.34), channel_id=1, source_target_pairs={{0,1},{1,0},{2,3},{3,2},{4,5},{5,4},{6,7},{7,6},{8,9},{9,8},{10,11... | collective-permute-start | bytes 1572872 | tf_op jit(solution)/shard_map/ppermute | solution.py:367
  38.8 0.7 %shard_map.114 = (f32[64,32,128]{2,1,0:T(8,128)S(1)}, bf16[64,32,128]{2,1,0:T(8,128)(2,1)S(1)}) custom-call(bf16[64,192]{1,0:T(8,128)(2,1)S(1)} %get-tuple-element.20.refs_3_.left, f32[8192,128]{1,0:T(8,128)S(1)} %get-tuple-element.30.acc), custom_call_target="tpu_custom_call" | custom-call | tf_op jit(solution)/shard_map/pallas_call | solution.py:368
  39.5 0.1 collective-permute-start.5
  39.6 0.8 %collective-permute-done.6.refs_1_ = bf16[64,32,128]{2,1,0:T(8,128)(2,1)S(1)} collective-permute-done((bf16[64,32,128]{2,1,0:T(8,128)(2,1)S(1)}, bf16[64,32,128]{2,1,0:T(8,128)(2,1)S(1)}, u32[]{:S(2)}, u32[]{:S(2)}) %collective-permute-start.6) | collective-permute-done | bytes 524320 | tf_op jit(solution)/shard_map/ppermute | solution.py:367
  40.4 1.0 %shard_map.115.refs_2_ = f32[32,128,128]{2,1,0:T(8,128)} custom-call(f32[64,32,128]{2,1,0:T(8,128)S(1)} %get-tuple-element.33.refs_0_, bf16[64,32,128]{2,1,0:T(8,128)(2,1)S(1)} %collective-permute-done.6.refs_1_), custom_call_target="tpu_custom_call" | custom-call | tf_op jit(solution)/shard_map/pallas_call | solution.py:315
  41.4 0.1 collective-permute-done.5.refs_1_
  41.5 1.0 %shard_map.116 = f32[32,128,128]{2,1,0:T(8,128)} custom-call(f32[64,32,128]{2,1,0:T(8,128)S(1)} %get-tuple-element.31.refs_0_, bf16[64,32,128]{2,1,0:T(8,128)(2,1)S(1)} %collective-permute-done.5.refs_1_, f32[32,128,128]{2,1,0:T(8,128)} %shard_map.115.refs_2_), custom_call_target="tpu_custom_call", output_to_operand_aliasing={{}: (2, {})} | custom-call | tf_op jit(solution)/shard_map/pallas_call | solution.py:315
  (2 shorter events, 0.0 us)
Async XLA Ops:
  1.9 6.5 %collective-permute-start.1 = (bf16[544,128]{1,0:T(8,128)(2,1)S(1)}, bf16[544,128]{1,0:T(8,128)(2,1)S(1)}, u32[]{:S(2)}, u32[]{:S(2)}) collective-permute-start(bf16[544,128]{1,0:T(8,128)(2,1)S(1)} %get-tuple-element.22.refs_1_), channel_id=1, source_target_pairs={{0,12},{2,14},{4,0},{6,2},{8,4},{10,6},{12,8},{14,10},{1,13},{3,15... | collective-permute-start | bytes 417800 | tf_op jit(solution)/shard_map/ppermute | solution.py:348
  2.1 6.3 %collective-permute-start = (bf16[544,128]{1,0:T(8,128)(2,1)S(1)}, bf16[544,128]{1,0:T(8,128)(2,1)S(1)}, u32[]{:S(2)}, u32[]{:S(2)}) collective-permute-start(bf16[544,128]{1,0:T(8,128)(2,1)S(1)} %get-tuple-element.22.refs_1_), channel_id=1, source_target_pairs={{0,4},{2,6},{4,8},{6,10},{8,12},{10,14},{12,0},{14,2},{1,5},{3,7},... | collective-permute-start | bytes 417800 | tf_op jit(solution)/shard_map/ppermute | solution.py:348
  8.4 16.3 %collective-permute-start.2 = (bf16[1088,128]{1,0:T(8,128)(2,1)S(1)}, bf16[1088,128]{1,0:T(8,128)(2,1)S(1)}, u32[]{:S(2)}, u32[]{:S(2)}) collective-permute-start(bf16[1088,128]{1,0:T(8,128)(2,1)S(1)} %constant_dynamic-update-slice_fusion.refs_2_), channel_id=1, source_target_pairs={{0,2},{2,0},{4,6},{6,4},{8,10},{10,8},{12,14},{14,12},{1,3},{3,1},... | collective-permute-start | bytes 835592 | tf_op jit(solution)/shard_map/ppermute | solution.py:348
  9.7 8.7 %collective-permute-start.4 = (bf16[544,128]{1,0:T(8,128)(2,1)S(1)}, bf16[544,128]{1,0:T(8,128)(2,1)S(1)}, u32[]{:S(2)}, u32[]{:S(2)}) collective-permute-start(bf16[544,128]{1,0:T(8,128)(2,1)S(1)} %get-tuple-element.22.refs_1_), channel_id=1, source_target_pairs={{0,2},{2,0},{4,6},{6,4},{8,10},{10,8},{12,14},{14,12},{1,3},{3,1},... | collective-permute-start | bytes 417800 | tf_op jit(solution)/shard_map/ppermute | solution.py:348
  9.9 14.6 %collective-permute-start.3 = (bf16[544,128]{1,0:T(8,128)(2,1)S(1)}, bf16[544,128]{1,0:T(8,128)(2,1)S(1)}, u32[]{:S(2)}, u32[]{:S(2)}) collective-permute-start(bf16[544,128]{1,0:T(8,128)(2,1)S(1)} %get-tuple-element.22.refs_1_), channel_id=1, source_target_pairs={{0,10},{2,8},{4,14},{6,12},{8,2},{10,0},{12,6},{14,4},{1,11},{3,9}... | collective-permute-start | bytes 417800 | tf_op jit(solution)/shard_map/ppermute | solution.py:348
  27.6 12.8 %collective-permute-start.6 = (bf16[64,32,128]{2,1,0:T(8,128)(2,1)S(1)}, bf16[64,32,128]{2,1,0:T(8,128)(2,1)S(1)}, u32[]{:S(2)}, u32[]{:S(2)}) collective-permute-start(bf16[64,32,128]{2,1,0:T(8,128)(2,1)S(1)} %get-tuple-element.34), channel_id=1, source_target_pairs={{0,1},{1,0},{2,3},{3,2},{4,5},{5,4},{6,7},{7,6},{8,9},{9,8},{10,11... | collective-permute-start | bytes 1572872 | tf_op jit(solution)/shard_map/ppermute | solution.py:367
  39.5 2.0 %collective-permute-start.5 = (bf16[64,32,128]{2,1,0:T(8,128)(2,1)S(1)}, bf16[64,32,128]{2,1,0:T(8,128)(2,1)S(1)}, u32[]{:S(2)}, u32[]{:S(2)}) collective-permute-start(bf16[64,32,128]{2,1,0:T(8,128)(2,1)S(1)} %get-tuple-element.32), channel_id=1, source_target_pairs={{0,1},{1,0},{2,3},{3,2},{4,5},{5,4},{6,7},{7,6},{8,9},{9,8},{10,11... | collective-permute-start | bytes 1572872 | tf_op jit(solution)/shard_map/ppermute | solution.py:378
where the time goes:
time: 42.6 us; the launch traced here: 42.5 us
  starting transfers between devices  20.4 us (48%)
  Pallas kernels  15.4 us (36%)
  waiting for transfers between devices  5.96 us (14%)
  between operations  0.74 us (2%)
    pallas_call x4, Pallas kernels, main_call(): pl.pallas_call(functools.partial(main_kernel, hops=hops, capacity=capacit...  11.5 us
    ppermute x1, starting transfers between devices, shards(): first_other = lax.ppermute(other, 'sect', [(0, 1), (1, 0)])  11.2 us
    ppermute x5, starting transfers between devices, move(): lax.ppermute(value, 'blk', [(i, where(i) % blocks) for i in range(blocks)])  9.07 us
    ppermute x5, waiting for transfers between devices, move(): lax.ppermute(value, 'blk', [(i, where(i) % blocks) for i in range(blocks)])  5.07 us
    pallas_call x2, Pallas kernels, finish(): pl.pallas_call(functools.partial(finish_kernel, base=base), out_shape=jax...  1.99 us
    pallas_call x1, Pallas kernels, pack(): pl.pallas_call(pack_kernel, out_shape=(jax.ShapeDtypeStruct((rows, TILE),...  1.19 us
  transfers between devices with their start and end apart: 7, of which 4 were waited for; matrix products, arithmetic and copies ran while one was open for 0% of the time, Pallas kernels for 24%

commit v1 on v0

--- a/solution.py
+++ b/solution.py
@@ -12,6 +12,7 @@
 TILE = 128
 JOIN = 2
 GROUP = 16
+BITS = 7
 F32 = jnp.float32
 BF16 = jnp.bfloat16
 VMEM = pl.BlockSpec(memory_space=pltpu.VMEM)
@@ -74,15 +75,16 @@
     fraction = frac_ref[0, 0].astype(F32)
     cell = cell_ref[0].astype(F32)
     level = level_ref[0].astype(F32)
+    live = (count + TILE - 1) // TILE
+    code = live + 8 * (reach_ref[0, 0] + 4 * reach_ref[0, 1])
+    lane = lax.broadcasted_iota(jnp.int32, (1, capacity), 1)
+    flag = jnp.where(lane < BITS, lax.shift_right_logical(code, jnp.minimum(lane, BITS)) & 1, 0)
+    cell = cell + (G_DEV * flag).astype(F32)
     rows = []
     for table in (fraction[0:1], fraction[1:2], cell, level):
         for i in range(chunks):
             rows.append(table[:, i * TILE : (i + 1) * TILE])
     out_ref[capacity : capacity + 4 * chunks, :] = jnp.concatenate(rows, 0).astype(BF16)
-    live = (count + TILE - 1) // TILE
-    code = live + 8 * (reach_ref[0, 0] + 4 * reach_ref[0, 1])
-    tail = out_ref.shape[0] - capacity - 4 * chunks
-    out_ref[capacity + 4 * chunks :, :] = jnp.full((tail, TILE), code, jnp.int32).astype(F32).astype(BF16)
     inv_x = 1.0 / lx_ref[...]
     inv_y = 1.0 / ly_ref[...]
     tilt = tl_ref[...]
@@ -104,7 +106,7 @@
 def pack(obs_count, reach, obs_weight, obs_frac, obs_cell, obs_level, scales, balance):
     capacity = obs_weight.shape[2]
     levels = balance.shape[0]
-    rows = capacity + 4 * (capacity // TILE) + 16
+    rows = capacity + 4 * (capacity // TILE)
     operands = [obs_count, reach, obs_weight, obs_frac, obs_cell, obs_level, *scales, balance]
     operands[1:] = [pltpu.with_memory_space_constraint(v, pltpu.HBM) for v in operands[1:]]
     spaces = [pltpu.SMEM] + [pltpu.VMEM] * 9
@@ -130,14 +132,17 @@
         w_all[i * capacity : (i + 1) * capacity, :] = packet[0:capacity, :]
         place = packet[capacity : capacity + 4 * chunks, :].astype(F32)
         fx, fy, cell, level = (place[t * chunks : (t + 1) * chunks] for t in range(4))
+        high = cell >= G_DEV
+        cell = jnp.where(high, cell - G_DEV, cell)
+        lane = lax.broadcasted_iota(jnp.int32, (chunks, TILE), 1)
+        weight = lax.shift_left(jnp.int32(1), jnp.minimum(lane, BITS)).astype(F32)
         cx = jnp.floor(cell * (1.0 / GY))
         cy = cell - cx * GY
         shift = jnp.full((1, TILE), offset, jnp.int32).astype(F32)
         ox_all[i * chunks : (i + 1) * chunks, :] = (cx + fx) * (1.0 / GX) - shift
         oy_all[i * chunks : (i + 1) * chunks, :] = (cy + fy) * (1.0 / GY)
         le_all[i * chunks : (i + 1) * chunks, :] = level
-        tail = packet[capacity + 4 * chunks :, :].astype(F32)
-        code = jnp.max(tail).astype(jnp.int32)
+        code = jnp.sum(jnp.where(high, weight, 0.0)).astype(jnp.int32)
         live = code & 7
         below = (code >> 3) & 3
         above = (code >> 5) & 3
@@ -230,7 +235,7 @@
     scale = refs.pop(0)
     if not first:
         refs.pop(0)
-    rows = capacity + 4 * (capacity // TILE) + 16
+    rows = capacity + 4 * (capacity // TILE)
     packets = []
     while len(packets) < len(hops):
         group = refs.pop(0)

time: 42.6 us -> 42.7 us (level)
  transfers between devices with their start and end apart: 7 -> 7, of which waited for: 4 -> 4; matrix products, arithmetic and copies ran while one was open for 0% -> 0% of each run, Pallas kernels for 24% -> 25%
where the time goes in v1:
time: 42.7 us; the launch traced here: 42.6 us
  starting transfers between devices  20.4 us (48%)
  Pallas kernels  15.8 us (37%)
  waiting for transfers between devices  5.66 us (13%)
  between operations  0.74 us (2%)
    pallas_call x4, Pallas kernels, main_call(): pl.pallas_call(functools.partial(main_kernel, hops=hops, capacity=capacit...  11.9 us
    ppermute x1, starting transfers between devices, shards(): first_other = lax.ppermute(other, 'sect', [(0, 1), (1, 0)])  11.3 us
    ppermute x5, starting transfers between devices, move(): lax.ppermute(value, 'blk', [(i, where(i) % blocks) for i in range(blocks)])  8.98 us
    ppermute x5, waiting for transfers between devices, move(): lax.ppermute(value, 'blk', [(i, where(i) % blocks) for i in range(blocks)])  4.77 us
    pallas_call x2, Pallas kernels, finish(): pl.pallas_call(functools.partial(finish_kernel, base=base), out_shape=jax...  1.99 us
    pallas_call x1, Pallas kernels, pack(): pl.pallas_call(pack_kernel, out_shape=(jax.ShapeDtypeStruct((rows, TILE),...  1.18 us
  transfers between devices with their start and end apart: 7, of which 4 were waited for; matrix products, arithmetic and copies ran while one was open for 0% of the time, Pallas kernels for 25%

profile of v1, /device:TPU:27, one launch (start us, length us, event | category | flops | bytes accessed | tf_op | source)
XLA Modules:
  0.0 42.6 jit_solution(18165867769170680862)
XLA Ops:
  0.7 1.2 %shard_map.109 = (bf16[528,128]{1,0:T(8,128)(2,1)S(1)}, f32[64,8]{1,0:T(8,128)S(1)}, bf16[64,192]{1,0:T(8,128)(2,1)S(1)}) custom-call(s32[1,1]{1,0:T(1,128)S(6)} %copy.21.count_ref, s32[1,2]{1,0:T(1,128)} %reach_hbm.1, bf16[1,1,512,128]{3,2,1,0:T(8,128)(2,1)} %weight_hbm.1, bf16[1,1,2,512]{3,2,1,0:T(2,128)(2,1)} %frac_hbm.1, s32[1,1,512]{2,1,0:T(1,128)} %cell_hbm.1, ...), custom_call_target="tpu_custom_call" | custom-call | tf_op jit(solution)/shard_map/pallas_call | solution.py:113
  1.8 0.2 collective-permute-start.1
  2.1 3.1 %collective-permute-start = (bf16[528,128]{1,0:T(8,128)(2,1)S(1)}, bf16[528,128]{1,0:T(8,128)(2,1)S(1)}, u32[]{:S(2)}, u32[]{:S(2)}) collective-permute-start(bf16[528,128]{1,0:T(8,128)(2,1)S(1)} %get-tuple-element.22.refs_1_), channel_id=1, source_target_pairs={{0,4},{2,6},{4,8},{6,10},{8,12},{10,14},{12,0},{14,2},{1,5},{3,7},... | collective-permute-start | bytes 405512 | tf_op jit(solution)/shard_map/ppermute | solution.py:353
  5.2 2.4 %shard_map.110.refs_1_ = f32[8192,128]{1,0:T(8,128)S(1)} custom-call(f32[64,8]{1,0:T(8,128)S(1)} %get-tuple-element.21.refs_0_, bf16[528,128]{1,0:T(8,128)(2,1)S(1)} %get-tuple-element.22.refs_1_), custom_call_target="tpu_custom_call" | custom-call | tf_op jit(solution)/shard_map/pallas_call | solution.py:283
  7.6 0.7 %collective-permute-done.1 = bf16[528,128]{1,0:T(8,128)(2,1)S(1)} collective-permute-done((bf16[528,128]{1,0:T(8,128)(2,1)S(1)}, bf16[528,128]{1,0:T(8,128)(2,1)S(1)}, u32[]{:S(2)}, u32[]{:S(2)}) %collective-permute-start.1) | collective-permute-done | bytes 135200 | tf_op jit(solution)/shard_map/ppermute | solution.py:353
  8.2 0.0 collective-permute-done
  8.3 1.3 %collective-permute-start.2 = (bf16[1056,128]{1,0:T(8,128)(2,1)S(1)}, bf16[1056,128]{1,0:T(8,128)(2,1)S(1)}, u32[]{:S(2)}, u32[]{:S(2)}) collective-permute-start(bf16[1056,128]{1,0:T(8,128)(2,1)S(1)} %constant_dynamic-update-slice_fusion.refs_2_), channel_id=1, source_target_pairs={{0,2},{2,0},{4,6},{6,4},{8,10},{10,8},{12,14},{14,12},{1,3},{3,1},... | collective-permute-start | bytes 811016 | tf_op jit(solution)/shard_map/ppermute | solution.py:353
  9.6 0.2 collective-permute-start.4
  9.8 4.1 %collective-permute-start.3 = (bf16[528,128]{1,0:T(8,128)(2,1)S(1)}, bf16[528,128]{1,0:T(8,128)(2,1)S(1)}, u32[]{:S(2)}, u32[]{:S(2)}) collective-permute-start(bf16[528,128]{1,0:T(8,128)(2,1)S(1)} %get-tuple-element.22.refs_1_), channel_id=1, source_target_pairs={{0,10},{2,8},{4,14},{6,12},{8,2},{10,0},{12,6},{14,4},{1,11},{3,9}... | collective-permute-start | bytes 405512 | tf_op jit(solution)/shard_map/ppermute | solution.py:353
  14.0 4.1 %collective-permute-done.4.refs_3_ = bf16[528,128]{1,0:T(8,128)(2,1)S(1)} collective-permute-done((bf16[528,128]{1,0:T(8,128)(2,1)S(1)}, bf16[528,128]{1,0:T(8,128)(2,1)S(1)}, u32[]{:S(2)}, u32[]{:S(2)}) %collective-permute-start.4) | collective-permute-done | bytes 135200 | tf_op jit(solution)/shard_map/ppermute | solution.py:353
  18.0 6.4 %shard_map.111.refs_1_ = f32[8192,128]{1,0:T(8,128)S(1)} custom-call(f32[64,8]{1,0:T(8,128)S(1)} %get-tuple-element.21.refs_0_, f32[8192,128]{1,0:T(8,128)S(1)} %shard_map.110.refs_1_, bf16[1056,128]{1,0:T(8,128)(2,1)S(1)} %constant_dynamic-update-slice_fusion.refs_2_, ...), custom_call_target="tpu_custom_call", output_to_operand_aliasing={{}: (1, {})} | custom-call | tf_op jit(solution)/shard_map/pallas_call | solution.py:283
  24.4 0.0 collective-permute-done.3.refs_2_
  24.5 0.1 shard_map.112.refs_1_
  24.6 0.0 collective-permute-done.2.refs_2_
  24.6 2.9 %shard_map.113 = (f32[8192,128]{1,0:T(8,128)S(1)}, f32[64,32,128]{2,1,0:T(8,128)S(1)}, bf16[64,32,128]{2,1,0:T(8,128)(2,1)S(1)}) custom-call(f32[64,8]{1,0:T(8,128)S(1)} %get-tuple-element.21.refs_0_, f32[8192,128]{1,0:T(8,128)S(1)} %shard_map.112.refs_1_, bf16[1056,128]{1,0:T(8,128)(2,1)S(1)} %collective-permute-done.2.refs_2_, ...), custom_call_target="tpu_custom_call", output_to_operand_aliasing={{0}: (1, {})} | custom-call | tf_op jit(solution)/shard_map/pallas_call | solution.py:283
  27.6 11.3 %collective-permute-start.6 = (bf16[64,32,128]{2,1,0:T(8,128)(2,1)S(1)}, bf16[64,32,128]{2,1,0:T(8,128)(2,1)S(1)}, u32[]{:S(2)}, u32[]{:S(2)}) collective-permute-start(bf16[64,32,128]{2,1,0:T(8,128)(2,1)S(1)} %get-tuple-element.34), channel_id=1, source_target_pairs={{0,1},{1,0},{2,3},{3,2},{4,5},{5,4},{6,7},{7,6},{8,9},{9,8},{10,11... | collective-permute-start | bytes 1572872 | tf_op jit(solution)/shard_map/ppermute | solution.py:372
  38.9 0.7 %shard_map.114 = (f32[64,32,128]{2,1,0:T(8,128)S(1)}, bf16[64,32,128]{2,1,0:T(8,128)(2,1)S(1)}) custom-call(bf16[64,192]{1,0:T(8,128)(2,1)S(1)} %get-tuple-element.20.refs_3_.left, f32[8192,128]{1,0:T(8,128)S(1)} %get-tuple-element.30.acc), custom_call_target="tpu_custom_call" | custom-call | tf_op jit(solution)/shard_map/pallas_call | solution.py:373
  39.6 0.1 collective-permute-start.5
  39.7 0.7 %collective-permute-done.6.refs_1_ = bf16[64,32,128]{2,1,0:T(8,128)(2,1)S(1)} collective-permute-done((bf16[64,32,128]{2,1,0:T(8,128)(2,1)S(1)}, bf16[64,32,128]{2,1,0:T(8,128)(2,1)S(1)}, u32[]{:S(2)}, u32[]{:S(2)}) %collective-permute-start.6) | collective-permute-done | bytes 524320 | tf_op jit(solution)/shard_map/ppermute | solution.py:372
  40.4 1.0 %shard_map.115.refs_2_ = f32[32,128,128]{2,1,0:T(8,128)} custom-call(f32[64,32,128]{2,1,0:T(8,128)S(1)} %get-tuple-element.33.refs_0_, bf16[64,32,128]{2,1,0:T(8,128)(2,1)S(1)} %collective-permute-done.6.refs_1_), custom_call_target="tpu_custom_call" | custom-call | tf_op jit(solution)/shard_map/pallas_call | solution.py:320
  41.4 0.2 collective-permute-done.5.refs_1_
  41.6 1.0 %shard_map.116 = f32[32,128,128]{2,1,0:T(8,128)} custom-call(f32[64,32,128]{2,1,0:T(8,128)S(1)} %get-tuple-element.31.refs_0_, bf16[64,32,128]{2,1,0:T(8,128)(2,1)S(1)} %collective-permute-done.5.refs_1_, f32[32,128,128]{2,1,0:T(8,128)} %shard_map.115.refs_2_), custom_call_target="tpu_custom_call", output_to_operand_aliasing={{}: (2, {})} | custom-call | tf_op jit(solution)/shard_map/pallas_call | solution.py:320
  (2 shorter events, 0.0 us)
Async XLA Ops:
  1.8 6.4 %collective-permute-start.1 = (bf16[528,128]{1,0:T(8,128)(2,1)S(1)}, bf16[528,128]{1,0:T(8,128)(2,1)S(1)}, u32[]{:S(2)}, u32[]{:S(2)}) collective-permute-start(bf16[528,128]{1,0:T(8,128)(2,1)S(1)} %get-tuple-element.22.refs_1_), channel_id=1, source_target_pairs={{0,12},{2,14},{4,0},{6,2},{8,4},{10,6},{12,8},{14,10},{1,13},{3,15... | collective-permute-start | bytes 405512 | tf_op jit(solution)/shard_map/ppermute | solution.py:353
  2.1 6.2 %collective-permute-start = (bf16[528,128]{1,0:T(8,128)(2,1)S(1)}, bf16[528,128]{1,0:T(8,128)(2,1)S(1)}, u32[]{:S(2)}, u32[]{:S(2)}) collective-permute-start(bf16[528,128]{1,0:T(8,128)(2,1)S(1)} %get-tuple-element.22.refs_1_), channel_id=1, source_target_pairs={{0,4},{2,6},{4,8},{6,10},{8,12},{10,14},{12,0},{14,2},{1,5},{3,7},... | collective-permute-start | bytes 405512 | tf_op jit(solution)/shard_map/ppermute | solution.py:353
  8.3 16.3 %collective-permute-start.2 = (bf16[1056,128]{1,0:T(8,128)(2,1)S(1)}, bf16[1056,128]{1,0:T(8,128)(2,1)S(1)}, u32[]{:S(2)}, u32[]{:S(2)}) collective-permute-start(bf16[1056,128]{1,0:T(8,128)(2,1)S(1)} %constant_dynamic-update-slice_fusion.refs_2_), channel_id=1, source_target_pairs={{0,2},{2,0},{4,6},{6,4},{8,10},{10,8},{12,14},{14,12},{1,3},{3,1},... | collective-permute-start | bytes 811016 | tf_op jit(solution)/shard_map/ppermute | solution.py:353
  9.6 8.4 %collective-permute-start.4 = (bf16[528,128]{1,0:T(8,128)(2,1)S(1)}, bf16[528,128]{1,0:T(8,128)(2,1)S(1)}, u32[]{:S(2)}, u32[]{:S(2)}) collective-permute-start(bf16[528,128]{1,0:T(8,128)(2,1)S(1)} %get-tuple-element.22.refs_1_), channel_id=1, source_target_pairs={{0,2},{2,0},{4,6},{6,4},{8,10},{10,8},{12,14},{14,12},{1,3},{3,1},... | collective-permute-start | bytes 405512 | tf_op jit(solution)/shard_map/ppermute | solution.py:353
  9.8 14.6 %collective-permute-start.3 = (bf16[528,128]{1,0:T(8,128)(2,1)S(1)}, bf16[528,128]{1,0:T(8,128)(2,1)S(1)}, u32[]{:S(2)}, u32[]{:S(2)}) collective-permute-start(bf16[528,128]{1,0:T(8,128)(2,1)S(1)} %get-tuple-element.22.refs_1_), channel_id=1, source_target_pairs={{0,10},{2,8},{4,14},{6,12},{8,2},{10,0},{12,6},{14,4},{1,11},{3,9}... | collective-permute-start | bytes 405512 | tf_op jit(solution)/shard_map/ppermute | solution.py:353
  27.6 12.9 %collective-permute-start.6 = (bf16[64,32,128]{2,1,0:T(8,128)(2,1)S(1)}, bf16[64,32,128]{2,1,0:T(8,128)(2,1)S(1)}, u32[]{:S(2)}, u32[]{:S(2)}) collective-permute-start(bf16[64,32,128]{2,1,0:T(8,128)(2,1)S(1)} %get-tuple-element.34), channel_id=1, source_target_pairs={{0,1},{1,0},{2,3},{3,2},{4,5},{5,4},{6,7},{7,6},{8,9},{9,8},{10,11... | collective-permute-start | bytes 1572872 | tf_op jit(solution)/shard_map/ppermute | solution.py:372
  39.6 2.0 %collective-permute-start.5 = (bf16[64,32,128]{2,1,0:T(8,128)(2,1)S(1)}, bf16[64,32,128]{2,1,0:T(8,128)(2,1)S(1)}, u32[]{:S(2)}, u32[]{:S(2)}) collective-permute-start(bf16[64,32,128]{2,1,0:T(8,128)(2,1)S(1)} %get-tuple-element.32), channel_id=1, source_target_pairs={{0,1},{1,0},{2,3},{3,2},{4,5},{5,4},{6,7},{7,6},{8,9},{9,8},{10,11... | collective-permute-start | bytes 1572872 | tf_op jit(solution)/shard_map/ppermute | solution.py:383
